TPU v7x, 256 devices: a whole 4x4x8 slice. The times are simulated.
256 devices in a mesh: dom: 32 (over x, z), cls: 8 (over y, core).
Axes of the slice: x: 4, y: 4, z: 8, core: 2. Of those that a mesh axis runs over, the one named last changes fastest.
Arguments:
- images: bfloat16 [3072, 13824], P('dom')
- pick_counts: int32 [32], replicated, may hold values from 0 to 96, as said below
- group_of: int32 [3072], replicated, may hold values from 0 to 31
- ctf_table: float32 [32, 32], replicated, may hold values from -1 to 1
- precision: float32 [32], replicated, may hold values from 0.1 to 1
- references: bfloat16 [200, 13824], P('cls')
Outputs:
- new_refs: float32 [200, 13824], P('cls', 'dom')
- confidence: float32 [3072], P('dom')
Inputs may be any that keep to these rules, and one draw needn't show every extreme that they name: `pick_counts`: the counts sum to 1536; each reader and the reader half of the dom axis away hold 96 particles together, and some reader holds exactly 96.
All inputs are finite; a program needn't handle non-finite values.
Results may differ from a plain program's by a relative error of at most 0.0037.
Values may be sent and summed in bfloat16 or wider, within the bound.
No kernel may reach another device: no remote copies, remote signals or barrier semaphores. Data moves between devices by JAX's collectives and lax.ppermute only.
A program may use at most 320 MiB of HBM per device.

v0:
```python
import functools

import jax
import jax.numpy as jnp
from jax import lax
from jax.experimental import pallas as pl
from jax.experimental.pallas import tpu as pltpu
from jax.sharding import PartitionSpec as P


CYCLES = 32
ANG = 216
STEP = 6
READ = 96
K_OWN = 25
GROUPS = 32

SPAN = 2 * ANG
HOP = 2 * STEP
N1 = 6
N2 = 6
CHUNKS = 4
CYC = 8
WIDE = CYC * SPAN
TILES = WIDE // 128
EDGE = SPAN - 384
QP = 128
KP = 32
LOW = 13
PACK = 3 * K_OWN + LOW

ridge_term = 0.02
HIGH = lax.Precision.HIGHEST
X_SIZE, Z_SIZE = 4, 8

VM = pl.BlockSpec(memory_space=pltpu.VMEM)
FAR = pl.BlockSpec(memory_space=pltpu.HBM)
PARAMS = pltpu.CompilerParams(vmem_limit_bytes=12 * 1024 * 1024)


def plan(sources):
    runs = []
    for lane, src in enumerate(sources):
        if src is None:
            continue
        key = (src // 128, (src - lane) % 128)
        if runs and runs[-1][2] == key and runs[-1][1] == lane:
            runs[-1][1] = lane + 1
        else:
            runs.append([lane, lane + 1, key])
    return sorted(runs, key=lambda run: run[0] - run[1])


def rolled_plan(shift):
    tiles = []
    for tile in range(TILES):
        sources = []
        for lane in range(128):
            cycle, place = divmod(128 * tile + lane, SPAN)
            sources.append(cycle * SPAN + (place + shift) % SPAN)
        tiles.append(plan(sources))
    return tiles


def packed_plan(cycle, part, shift):
    sources = []
    for lane in range(128):
        place = 128 * part + lane
        sources.append(cycle * SPAN + (place + shift) % SPAN if place < SPAN else None)
    return plan(sources)


def gather_tile(runs, load, lane, cache):
    value = None
    for first, last, (tile, turn) in runs:
        key = (tile, turn)
        if key not in cache:
            piece = load(tile)
            cache[key] = pltpu.roll(piece, 128 - turn, axis=1) if turn else piece
        piece = cache[key]
        if value is None:
            value = piece
            continue
        if first == 0:
            mask = lane < last
        elif last == 128:
            mask = lane >= first
        else:
            mask = (lane >= first) & (lane < last)
        value = jnp.where(mask, piece, value)
    return value


def match_kernel(
    images,
    refs,
    groups_far,
    table_far,
    precision_far,
    counts_far,
    stack,
    prob,
    stats,
    power_out,
    pix,
    raw,
    turned,
    scales,
    logits,
    groups,
    table,
    precision,
    counts,
    sems,
    small_sems,
):
    me = lax.axis_index("dom")
    small = [
        pltpu.make_async_copy(src, dst, small_sems.at[n])
        for n, (src, dst) in enumerate(
            (
                (groups_far, groups),
                (table_far, table),
                (precision_far, precision),
                (counts_far, counts),
            )
        )
    ]
    for copy in small:
        copy.start()
    copies = []
    for i in range(CHUNKS):
        span = pl.ds(i * WIDE, WIDE)
        copies.append(pltpu.make_async_copy(refs.at[:, span], raw.at[i], sems.at[0, i]))
        copies.append(pltpu.make_async_copy(images.at[:, span], pix.at[i], sems.at[1, i]))
    for copy in copies:
        copy.start()
    for copy in small:
        copy.wait()

    lane = lax.broadcasted_iota(jnp.int32, (8, QP), 1)
    base = me * READ
    row = base // 128
    off = base - row * 128
    turn = lax.rem(128 - off, 128)
    head = jnp.broadcast_to(groups[pl.ds(row, 1), :], (8, QP))
    tail = jnp.broadcast_to(groups[pl.ds(jnp.minimum(row + 1, 23), 1), :], (8, QP))
    mine = jnp.where(
        lane + off < 128, pltpu.roll(head, turn, axis=1), pltpu.roll(tail, turn, axis=1)
    )
    hot = (lax.broadcasted_iota(jnp.int32, (QP, QP), 0) == mine[0:1, :]).astype(jnp.float32)
    hot = hot.T[:, :GROUPS]
    ctf = jnp.dot(hot, table[...], precision=HIGH, preferred_element_type=jnp.float32)
    scale = precision[...] * ctf
    power = precision[...] * jnp.square(ctf)
    power_out[...] = power
    for i in range(CHUNKS):
        scales[i, :, 0:CYC] = scale[:, i * CYC : (i + 1) * CYC]

    logits[...] = jnp.zeros_like(logits)

    def chunk_step(i, energy):
        pltpu.make_async_copy(refs.at[:, pl.ds(0, WIDE)], raw.at[i], sems.at[0, i]).wait()
        lane_r = lax.broadcasted_iota(jnp.int32, (K_OWN, 128), 1)
        tiles = [raw[i, :, 128 * t : 128 * t + 128] for t in range(TILES)]
        for r2 in range(N2):
            cache = {}
            plans = rolled_plan((SPAN - N1 * HOP * r2) % SPAN)
            for t in range(TILES):
                turned[r2 * KP : r2 * KP + K_OWN, 128 * t : 128 * t + 128] = gather_tile(
                    plans[t], lambda u: tiles[u], lane_r, cache
                )
        lane_e = lax.broadcasted_iota(jnp.int32, (K_OWN, CYCLES), 1)
        sums = [None] * CYC
        for t in range(TILES):
            square = jnp.square(tiles[t].astype(jnp.float32))
            lo, hi = 128 * t // SPAN, (128 * t + 127) // SPAN
            parts = [(lo, square)]
            if hi != lo:
                edge = hi * SPAN - 128 * t
                parts = [
                    (lo, jnp.where(lane_r < edge, square, 0.0)),
                    (hi, jnp.where(lane_r >= edge, square, 0.0)),
                ]
            for c, part in parts:
                sums[c] = part if sums[c] is None else sums[c] + part
        for c in range(CYC):
            total = jnp.sum(sums[c], axis=1, keepdims=True)
            energy = jnp.where(lane_e == i * CYC + c, total, energy)

        pltpu.make_async_copy(images.at[:, pl.ds(0, WIDE)], pix.at[i], sems.at[1, i]).wait()
        for r1 in range(N1):
            stack[i, r1 * QP + READ : (r1 + 1) * QP, :] = jnp.zeros(
                (QP - READ, WIDE), jnp.bfloat16
            )

        def row_step(j, carry):
            rows = pl.ds(pl.multiple_of(j * 16, 16), 16)
            lane_w = lax.broadcasted_iota(jnp.int32, (16, 128), 1)
            factor = scales[i, rows, :]
            cols = [jnp.broadcast_to(factor[:, c : c + 1], (16, 128)) for c in range(CYC)]
            weighted = []
            for t in range(TILES):
                lo, hi = 128 * t // SPAN, (128 * t + 127) // SPAN
                amount = cols[lo]
                if hi != lo:
                    amount = jnp.where(lane_w < hi * SPAN - 128 * t, cols[lo], cols[hi])
                pixels = pix[i, rows, 128 * t : 128 * t + 128].astype(jnp.float32)
                weighted.append((amount * pixels).astype(jnp.bfloat16))
            for r1 in range(N1):
                cache = {}
                plans = rolled_plan(HOP * r1)
                out_rows = pl.ds(pl.multiple_of(r1 * QP + j * 16, 16), 16)
                for t in range(TILES):
                    stack[i, out_rows, 128 * t : 128 * t + 128] = gather_tile(
                        plans[t], lambda u: weighted[u], lane_w, cache
                    )
            return carry

        lax.fori_loop(0, READ // 16, row_step, 0)
        logits[...] += lax.dot_general(
            turned[...], stack[i], (((1,), (1,)), ((), ())), preferred_element_type=jnp.float32
        )
        return energy

    energy = lax.fori_loop(0, CHUNKS, chunk_step, jnp.zeros((K_OWN, CYCLES), jnp.float32))
    ref_power = lax.dot_general(
        energy,
        power,
        (((1,), (1,)), ((), ())),
        precision=HIGH,
        preferred_element_type=jnp.float32,
    )
    half = 0.5 * ref_power
    lane_q = lax.broadcasted_iota(jnp.int32, (K_OWN, QP), 1)
    alive = lane_q < counts[me]
    peak = jnp.full((K_OWN, QP), -3.0e38, jnp.float32)
    for r2 in range(N2):
        for r1 in range(N1):
            rows = slice(r2 * KP, r2 * KP + K_OWN)
            cols = slice(r1 * QP, (r1 + 1) * QP)
            value = jnp.where(alive, logits[rows, cols] - half, 0.0)
            logits[rows, cols] = value
            peak = jnp.maximum(peak, value)
    peak = jnp.max(peak, axis=0, keepdims=True)
    mass = jnp.zeros((K_OWN, QP), jnp.float32)
    prob[...] = jnp.zeros_like(prob)
    for r2 in range(N2):
        for r1 in range(N1):
            rows = slice(r2 * KP, r2 * KP + K_OWN)
            cols = slice(r1 * QP, (r1 + 1) * QP)
            value = jnp.exp(logits[rows, cols] - peak)
            prob[rows, cols] = value
            mass = mass + value
    mass = jnp.sum(mass, axis=0, keepdims=True)
    sub = lax.broadcasted_iota(jnp.int32, (8, QP), 0)
    block = jnp.where(sub == 0, peak, jnp.where(alive[0:1, :], mass, 0.0))
    for i in range(8):
        stats[i] = block


def scatter_chunk(stack, post, dens, partial, out, x_to):
    partial[...] = jnp.dot(post[...], stack[x_to], preferred_element_type=jnp.float32)
    lane = lax.broadcasted_iota(jnp.int32, (KP, 128), 1)
    caches = [{} for _ in range(N2)]
    for c in range(CYC):
        for part in range(4):
            total = None
            for r2 in range(N2):
                value = gather_tile(
                    packed_plan(c, part, N1 * HOP * r2),
                    lambda u: partial[r2 * KP : (r2 + 1) * KP, 128 * u : 128 * u + 128],
                    lane,
                    caches[r2],
                )
                total = value if total is None else total + value
            if part == 3:
                total = jnp.where(lane == EDGE, dens[x_to][:, c : c + 1], total)
                high = pltpu.roll(total[LOW : 2 * LOW], 64, axis=1)
                total = jnp.where(lane[:LOW] < 64, total[:LOW], high)
                out[c, 3 * K_OWN : PACK, :] = total.astype(out.dtype)
            else:
                out[c, K_OWN * part : K_OWN * (part + 1), :] = total[:K_OWN].astype(out.dtype)


def first_chunk_kernel(
    hop, stack, prob, stats, power, out, post, dens, conf, partial
):
    me = lax.axis_index("dom")
    seat = lax.axis_index("cls")
    peak = stats[0][0:1, :]
    for i in range(1, 8):
        peak = jnp.maximum(peak, stats[i][0:1, :])
    mass = jnp.zeros((1, QP), jnp.float32)
    for i in range(8):
        mass = mass + stats[i][1:2, :] * jnp.exp(stats[i][0:1, :] - peak)
    alive = mass > 0.0
    own_peak = stats[seat][0:1, :]
    factor = jnp.where(alive, jnp.exp(own_peak - peak) / mass, 0.0)
    conf[...] = jnp.where(alive, 1.0 / mass, 0.0)[:, :READ]
    total = jnp.zeros((KP, QP), jnp.float32)
    for r2 in range(N2):
        for r1 in range(N1):
            rows = slice(r2 * KP, (r2 + 1) * KP)
            cols = slice(r1 * QP, (r1 + 1) * QP)
            value = prob[rows, cols] * factor
            total = total + value
            post[rows, cols] = value.astype(jnp.bfloat16)
    den = jnp.dot(total, power[...], precision=HIGH, preferred_element_type=jnp.float32)
    for i in range(CHUNKS):
        dens[i, :, 0:CYC] = den[:, i * CYC : (i + 1) * CYC]
    scatter_chunk(stack, post, dens, partial, out, lax.rem(me // Z_SIZE + hop, X_SIZE))


def chunk_kernel(hop, stack, post, dens, out, partial):
    me = lax.axis_index("dom")
    scatter_chunk(stack, post, dens, partial, out, lax.rem(me // Z_SIZE + hop, X_SIZE))


def finish_kernel(pieces, out, acc):
    total = pieces[0].astype(jnp.float32)
    for i in range(1, Z_SIZE):
        total = total + pieces[i].astype(jnp.float32)
    acc[...] = total
    low = acc[3 * K_OWN : PACK, :]
    high = acc[3 * K_OWN : 4 * K_OWN - LOW, 64:128]
    den_low = low[:, EDGE : EDGE + 1] + ridge_term
    den_high = high[:, EDGE : EDGE + 1] + ridge_term
    den = jnp.concatenate([den_low, den_high], axis=0)
    for part in range(3):
        out[:, 128 * part : 128 * (part + 1)] = acc[K_OWN * part : K_OWN * (part + 1), :] / den
    out[0:LOW, 384:SPAN] = low[:, 0:EDGE] / den_low
    out[LOW:K_OWN, 384:SPAN] = high[:, 0:EDGE] / den_high


def in_hbm(x):
    return pltpu.with_memory_space_constraint(x, pltpu.HBM)


def in_vmem(x):
    return pltpu.with_memory_space_constraint(x, pltpu.VMEM)


def body(images, pick_counts, group_of, ctf_table, precision, references):
    f32, bf16 = jnp.float32, jnp.bfloat16
    operands = (
        images,
        references,
        group_of.reshape(24, 128),
        ctf_table,
        precision.reshape(1, CYCLES),
        pick_counts,
    )
    stack, prob, stats, power = pl.pallas_call(
        match_kernel,
        out_shape=(
            pltpu.VMEM((CHUNKS, N1 * QP, WIDE), bf16),
            pltpu.VMEM((N2 * KP, N1 * QP), f32),
            jax.ShapeDtypeStruct((8, 8, QP), f32),
            pltpu.VMEM((QP, CYCLES), f32),
        ),
        in_specs=[FAR] * 6,
        out_specs=(VM, VM, VM, VM),
        scratch_shapes=[
            pltpu.VMEM((CHUNKS, READ, WIDE), bf16),
            pltpu.VMEM((CHUNKS, K_OWN, WIDE), bf16),
            pltpu.VMEM((N2 * KP, WIDE), bf16),
            pltpu.VMEM((CHUNKS, QP, 128), f32),
            pltpu.VMEM((N2 * KP, N1 * QP), f32),
            pltpu.VMEM((24, 128), jnp.int32),
            pltpu.VMEM((GROUPS, CYCLES), f32),
            pltpu.VMEM((1, CYCLES), f32),
            pltpu.SMEM((32,), jnp.int32),
            pltpu.SemaphoreType.DMA((2, CHUNKS)),
            pltpu.SemaphoreType.DMA((4,)),
        ],
        compiler_params=PARAMS,
        name="match",
    )(*map(in_hbm, operands))
    stats = lax.all_to_all(stats, "cls", 0, 0)
    stack, prob, power = in_vmem(stack), in_vmem(prob), in_vmem(power)

    part_shape = (CYC, PACK, 128)
    partial = pltpu.VMEM((N2 * KP, WIDE), f32)
    across, post, dens, conf = pl.pallas_call(
        functools.partial(first_chunk_kernel, 2),
        out_shape=(
            jax.ShapeDtypeStruct(part_shape, bf16),
            pltpu.VMEM((N2 * KP, N1 * QP), bf16),
            pltpu.VMEM((CHUNKS, KP, 128), f32),
            jax.ShapeDtypeStruct((1, READ), f32),
        ),
        in_specs=[VM, VM, VM, VM],
        out_specs=(VM, VM, VM, VM),
        scratch_shapes=[partial],
        compiler_params=PARAMS,
        name="chunk2",
    )(stack, prob, stats, power)
    post, dens = in_vmem(post), in_vmem(dens)

    def moved(piece, hop):
        ring = [(j, (j // Z_SIZE + hop) % X_SIZE * Z_SIZE + j % Z_SIZE) for j in range(32)]
        return lax.ppermute(piece, "dom", ring)

    def chunk_call(hop, dtype):
        return pl.pallas_call(
            functools.partial(chunk_kernel, hop),
            out_shape=jax.ShapeDtypeStruct(part_shape, dtype),
            in_specs=[VM, VM, VM],
            out_specs=VM,
            scratch_shapes=[partial],
            compiler_params=PARAMS,
        )(stack, post, dens)

    got2 = moved(across, 2)
    got1 = moved(chunk_call(1, bf16), 1)
    got3 = moved(chunk_call(3, bf16), 3)
    own = chunk_call(0, f32)
    total = own + got1.astype(f32) + got2.astype(f32) + got3.astype(f32)
    z_groups = [[x * Z_SIZE + z for z in range(Z_SIZE)] for x in range(X_SIZE)]
    pieces = lax.all_to_all(total.astype(bf16), "dom", 0, 0, axis_index_groups=z_groups)
    new_refs = pl.pallas_call(
        finish_kernel,
        out_shape=jax.ShapeDtypeStruct((K_OWN, SPAN), f32),
        in_specs=[VM],
        out_specs=VM,
        scratch_shapes=[pltpu.VMEM((PACK, 128), f32)],
        compiler_params=PARAMS,
        name="finish",
    )(pieces)
    return new_refs, conf.reshape(READ)


def solution(mesh):
    return jax.shard_map(
        body,
        mesh=mesh,
        in_specs=(P("dom", None), P(), P(), P(), P(), P("cls", None)),
        out_specs=(P("cls", "dom"), P("dom")),
        check_vma=False,
    )
```

profile of v0, /device:TPU:8, one launch (start us, length us, event | category | flops | bytes accessed | tf_op | source)
XLA Modules:
  0.0 65.6 jit_solution(1947511930880366399)
XLA Ops:
  0.6 19.6 %match.1 = (bf16[4,768,3456]{2,1,0:T(8,128)(2,1)S(1)}, f32[192,768]{1,0:T(8,128)S(1)}, f32[8,8,128]{2,1,0:T(8,128)S(1)}, f32[128,32]{1,0:T(8,128)S(1)}) custom-call(bf16[96,13824]{1,0:T(8,128)(2,1)} %images.1, bf16[25,13824]{1,0:T(8,128)(2,1)} %refs.1, s32[24,128]{1,0:T(8,128)} %bitcast.3, f32[32,32]{1,0:T(8,128)} %table_far.1, f32[1,32]{1,0:T(1,128)} %bitcast.4, ...), custom_call_target="tpu_custom_call" | custom-call | tf_op jit(solution)/shard_map/match/pallas_call | solution.py:354
  20.3 8.7 %all_to_all.10.stats = f32[8,8,128]{2,1,0:T(8,128)S(1)} all-to-all(f32[8,8,128]{2,1,0:T(8,128)S(1)} %get-tuple-element.12), channel_id=1, replica_groups=mesh['dom'=32,'cls'=8] {'cls'}, dimensions={0} | all-to-all | bytes 65536 | tf_op jit(solution)/shard_map/all_to_all | solution.py:380
  29.0 2.2 %chunk2.1 = (bf16[8,88,128]{2,1,0:T(8,128)(2,1)S(1)}, bf16[192,768]{1,0:T(8,128)(2,1)S(1)}, f32[4,32,128]{2,1,0:T(8,128)S(1)}, f32[1,96]{1,0:T(1,128)}) custom-call(bf16[4,768,3456]{2,1,0:T(8,128)(2,1)S(1)} %get-tuple-element.10.stack, f32[192,768]{1,0:T(8,128)S(1)} %get-tuple-element.11.prob, f32[8,8,128]{2,1,0:T(8,128)S(1)} %all_to_all.10.stats, ...), custom_call_target="tpu_custom_call" | custom-call | tf_op jit(solution)/shard_map/chunk2/pallas_call | solution.py:385
  31.1 1.7 %shard_map.79 = bf16[8,88,128]{2,1,0:T(8,128)(2,1)S(1)} custom-call(bf16[4,768,3456]{2,1,0:T(8,128)(2,1)S(1)} %get-tuple-element.10.stack, bf16[192,768]{1,0:T(8,128)(2,1)S(1)} %get-tuple-element.14.post, f32[4,32,128]{2,1,0:T(8,128)S(1)} %get-tuple-element.15.dens), custom_call_target="tpu_custom_call" | custom-call | tf_op jit(solution)/shard_map/pallas_call | solution.py:406
  32.8 1.7 %shard_map.78 = bf16[8,88,128]{2,1,0:T(8,128)(2,1)S(1)} custom-call(bf16[4,768,3456]{2,1,0:T(8,128)(2,1)S(1)} %get-tuple-element.10.stack, bf16[192,768]{1,0:T(8,128)(2,1)S(1)} %get-tuple-element.14.post, f32[4,32,128]{2,1,0:T(8,128)S(1)} %get-tuple-element.15.dens), custom_call_target="tpu_custom_call" | custom-call | tf_op jit(solution)/shard_map/pallas_call | solution.py:406
  34.5 1.6 %collective-permute-start = (bf16[8,88,128]{2,1,0:T(8,128)(2,1)S(1)}, bf16[8,88,128]{2,1,0:T(8,128)(2,1)S(1)}, u32[]{:S(2)}, u32[]{:S(2)}) collective-permute-start(bf16[8,88,128]{2,1,0:T(8,128)(2,1)S(1)} %shard_map.78), channel_id=1, source_target_pairs={{0,64},{8,72},{16,80},{24,88},{32,96},{40,104},{48,112},{56,120},{... | collective-permute-start | bytes 540680 | tf_op jit(solution)/shard_map/ppermute | solution.py:403
  36.0 1.7 %collective-permute-start.2 = (bf16[8,88,128]{2,1,0:T(8,128)(2,1)S(1)}, bf16[8,88,128]{2,1,0:T(8,128)(2,1)S(1)}, u32[]{:S(2)}, u32[]{:S(2)}) collective-permute-start(bf16[8,88,128]{2,1,0:T(8,128)(2,1)S(1)} %shard_map.79), channel_id=1, source_target_pairs={{0,192},{8,200},{16,208},{24,216},{32,224},{40,232},{48,240},{56,2... | collective-permute-start | bytes 540680 | tf_op jit(solution)/shard_map/ppermute | solution.py:403
  37.8 1.8 %collective-permute-start.1 = (bf16[8,88,128]{2,1,0:T(8,128)(2,1)S(1)}, bf16[8,88,128]{2,1,0:T(8,128)(2,1)S(1)}, u32[]{:S(2)}, u32[]{:S(2)}) collective-permute-start(bf16[8,88,128]{2,1,0:T(8,128)(2,1)S(1)} %get-tuple-element.16), channel_id=1, source_target_pairs={{0,128},{8,136},{16,144},{24,152},{32,160},{40,168},{48,176},{56,1... | collective-permute-start | bytes 540680 | tf_op jit(solution)/shard_map/ppermute | solution.py:403
  39.6 1.7 %shard_map.77 = f32[8,88,128]{2,1,0:T(8,128)S(1)} custom-call(bf16[4,768,3456]{2,1,0:T(8,128)(2,1)S(1)} %get-tuple-element.10.stack, bf16[192,768]{1,0:T(8,128)(2,1)S(1)} %get-tuple-element.14.post, f32[4,32,128]{2,1,0:T(8,128)S(1)} %get-tuple-element.15.dens), custom_call_target="tpu_custom_call" | custom-call | tf_op jit(solution)/shard_map/pallas_call | solution.py:406
  41.3 0.9 %collective-permute-done = bf16[8,88,128]{2,1,0:T(8,128)(2,1)S(1)} collective-permute-done((bf16[8,88,128]{2,1,0:T(8,128)(2,1)S(1)}, bf16[8,88,128]{2,1,0:T(8,128)(2,1)S(1)}, u32[]{:S(2)}, u32[]{:S(2)}) %collective-permute-start) | collective-permute-done | bytes 180256 | tf_op jit(solution)/shard_map/ppermute | solution.py:403
  42.2 1.3 %collective-permute-done.2 = bf16[8,88,128]{2,1,0:T(8,128)(2,1)S(1)} collective-permute-done((bf16[8,88,128]{2,1,0:T(8,128)(2,1)S(1)}, bf16[8,88,128]{2,1,0:T(8,128)(2,1)S(1)}, u32[]{:S(2)}, u32[]{:S(2)}) %collective-permute-start.2) | collective-permute-done | bytes 180256 | tf_op jit(solution)/shard_map/ppermute | solution.py:403
  43.5 3.4 %collective-permute-done.1 = bf16[8,88,128]{2,1,0:T(8,128)(2,1)S(1)} collective-permute-done((bf16[8,88,128]{2,1,0:T(8,128)(2,1)S(1)}, bf16[8,88,128]{2,1,0:T(8,128)(2,1)S(1)}, u32[]{:S(2)}, u32[]{:S(2)}) %collective-permute-start.1) | collective-permute-done | bytes 180256 | tf_op jit(solution)/shard_map/ppermute | solution.py:403
  46.8 0.1 add_convert_fusion
  46.9 17.9 %all_to_all.11.pieces = bf16[8,88,128]{2,1,0:T(8,128)(2,1)S(1)} all-to-all(bf16[8,88,128]{2,1,0:T(8,128)(2,1)S(1)} %add_convert_fusion), channel_id=1, replica_groups={{0,8,16,24,32,40,48,56},{64,72,80,88,96,104,112,120},{128,136,144,152,1..., dimensions={0} | all-to-all | bytes 360448 | tf_op jit(solution)/shard_map/all_to_all | solution.py:421
  64.8 0.8 %finish.1 = f32[25,432]{1,0:T(8,128)} custom-call(bf16[8,88,128]{2,1,0:T(8,128)(2,1)S(1)} %all_to_all.11.pieces), custom_call_target="tpu_custom_call" | custom-call | tf_op jit(solution)/shard_map/finish/pallas_call | solution.py:422
Async XLA Ops:
  34.5 7.7 %collective-permute-start = (bf16[8,88,128]{2,1,0:T(8,128)(2,1)S(1)}, bf16[8,88,128]{2,1,0:T(8,128)(2,1)S(1)}, u32[]{:S(2)}, u32[]{:S(2)}) collective-permute-start(bf16[8,88,128]{2,1,0:T(8,128)(2,1)S(1)} %shard_map.78), channel_id=1, source_target_pairs={{0,64},{8,72},{16,80},{24,88},{32,96},{40,104},{48,112},{56,120},{... | collective-permute-start | bytes 540680 | tf_op jit(solution)/shard_map/ppermute | solution.py:403
  36.0 7.4 %collective-permute-start.2 = (bf16[8,88,128]{2,1,0:T(8,128)(2,1)S(1)}, bf16[8,88,128]{2,1,0:T(8,128)(2,1)S(1)}, u32[]{:S(2)}, u32[]{:S(2)}) collective-permute-start(bf16[8,88,128]{2,1,0:T(8,128)(2,1)S(1)} %shard_map.79), channel_id=1, source_target_pairs={{0,192},{8,200},{16,208},{24,216},{32,224},{40,232},{48,240},{56,2... | collective-permute-start | bytes 540680 | tf_op jit(solution)/shard_map/ppermute | solution.py:403
  37.8 9.1 %collective-permute-start.1 = (bf16[8,88,128]{2,1,0:T(8,128)(2,1)S(1)}, bf16[8,88,128]{2,1,0:T(8,128)(2,1)S(1)}, u32[]{:S(2)}, u32[]{:S(2)}) collective-permute-start(bf16[8,88,128]{2,1,0:T(8,128)(2,1)S(1)} %get-tuple-element.16), channel_id=1, source_target_pairs={{0,128},{8,136},{16,144},{24,152},{32,160},{40,168},{48,176},{56,1... | collective-permute-start | bytes 540680 | tf_op jit(solution)/shard_map/ppermute | solution.py:403
where the time goes:
time: 66.4 us; the launch traced here: 65.6 us
  Pallas kernels  27.6 us (42%)
  blocking collectives  26.6 us (40%)
  waiting for transfers between devices  5.55 us (8%)
  starting transfers between devices  5.12 us (8%)
    pallas_call x1, Pallas kernels, body(): pl.pallas_call(match_kernel, out_shape=(pltpu.VMEM((CHUNKS, N1 * QP, WIDE...  19.6 us
    all_to_all x1, blocking collectives, body(): lax.all_to_all(total.astype(bf16), 'dom', 0, 0, axis_index_groups=z_groups)  17.9 us
    all_to_all x1, blocking collectives, body(): stats = lax.all_to_all(stats, 'cls', 0, 0)  8.7 us
    ppermute x3, waiting for transfers between devices, moved(): return lax.ppermute(piece, 'dom', ring)  5.55 us
    ppermute x3, starting transfers between devices, moved(): return lax.ppermute(piece, 'dom', ring)  5.12 us
    pallas_call x3, Pallas kernels, chunk_call(): pl.pallas_call(functools.partial(chunk_kernel, hop), out_shape=jax.ShapeD...  5.03 us
    pallas_call x1, Pallas kernels, body(): pl.pallas_call(functools.partial(first_chunk_kernel, 2), out_shape=(jax.S...  2.19 us
  transfers between devices with their start and end apart: 3, of which 3 were waited for; matrix products, arithmetic and copies ran while one was open for 0% of the time, Pallas kernels for 3%

commit v1 on v0

--- a/solution.py
+++ b/solution.py
@@ -70,7 +70,20 @@
     return plan(sources)
 
 
-def gather_tile(runs, load, lane, cache):
+def lane_mask(first, last, lane, masks):
+    if (first, last) not in masks:
+        low, high = jnp.asarray(first, lane.dtype), jnp.asarray(last, lane.dtype)
+        if first == 0:
+            mask = lane < high
+        elif last == 128:
+            mask = lane >= low
+        else:
+            mask = (lane >= low) & (lane < high)
+        masks[first, last] = mask
+    return masks[first, last]
+
+
+def gather_tile(runs, load, lane, cache, masks):
     value = None
     for first, last, (tile, turn) in runs:
         key = (tile, turn)
@@ -80,15 +93,22 @@
         piece = cache[key]
         if value is None:
             value = piece
-            continue
-        if first == 0:
-            mask = lane < last
-        elif last == 128:
-            mask = lane >= first
         else:
-            mask = (lane >= first) & (lane < last)
-        value = jnp.where(mask, piece, value)
+            value = jnp.where(lane_mask(first, last, lane, masks), piece, value)
     return value
+
+
+def store_tiles(ref, row_groups, plans, load, lane):
+    caches = [{} for _ in row_groups]
+    for t in range(0, TILES, 2):
+        masks = {}
+        for g, rows in enumerate(row_groups):
+            values = [
+                gather_tile(plans[u], functools.partial(load, g), lane, caches[g], masks)
+                for u in range(t, min(t + 2, TILES))
+            ]
+            wide = jnp.concatenate(values, axis=1) if len(values) > 1 else values[0]
+            ref[rows, 128 * t : 128 * t + wide.shape[1]] = wide
 
 
 def match_kernel(
@@ -157,20 +177,19 @@
     for i in range(CHUNKS):
         scales[i, :, 0:CYC] = scale[:, i * CYC : (i + 1) * CYC]
 
-    logits[...] = jnp.zeros_like(logits)
-
-    def chunk_step(i, energy):
-        pltpu.make_async_copy(refs.at[:, pl.ds(0, WIDE)], raw.at[i], sems.at[0, i]).wait()
-        lane_r = lax.broadcasted_iota(jnp.int32, (K_OWN, 128), 1)
+    lane_r = lax.broadcasted_iota(jnp.int32, (K_OWN, 128), 1)
+    lane_e = lax.broadcasted_iota(jnp.int32, (K_OWN, CYCLES), 1)
+    lane_w = lax.broadcasted_iota(jnp.int32, (16, 128), 1)
+    nought = [jnp.minimum(counts[i], 0) for i in range(CHUNKS)]
+
+    def turn_refs(i, energy):
+        copies[2 * i].wait()
         tiles = [raw[i, :, 128 * t : 128 * t + 128] for t in range(TILES)]
+        lane16 = (lane_r + nought[i]).astype(jnp.int16)
         for r2 in range(N2):
-            cache = {}
             plans = rolled_plan((SPAN - N1 * HOP * r2) % SPAN)
-            for t in range(TILES):
-                turned[r2 * KP : r2 * KP + K_OWN, 128 * t : 128 * t + 128] = gather_tile(
-                    plans[t], lambda u: tiles[u], lane_r, cache
-                )
-        lane_e = lax.broadcasted_iota(jnp.int32, (K_OWN, CYCLES), 1)
+            rows = [slice(r2 * KP, r2 * KP + K_OWN)]
+            store_tiles(turned.at[i % 2], rows, plans, lambda g, u: tiles[u], lane16)
         sums = [None] * CYC
         for t in range(TILES):
             square = jnp.square(tiles[t].astype(jnp.float32))
@@ -187,16 +206,12 @@
         for c in range(CYC):
             total = jnp.sum(sums[c], axis=1, keepdims=True)
             energy = jnp.where(lane_e == i * CYC + c, total, energy)
-
-        pltpu.make_async_copy(images.at[:, pl.ds(0, WIDE)], pix.at[i], sems.at[1, i]).wait()
-        for r1 in range(N1):
-            stack[i, r1 * QP + READ : (r1 + 1) * QP, :] = jnp.zeros(
-                (QP - READ, WIDE), jnp.bfloat16
-            )
-
-        def row_step(j, carry):
-            rows = pl.ds(pl.multiple_of(j * 16, 16), 16)
-            lane_w = lax.broadcasted_iota(jnp.int32, (16, 128), 1)
+        return energy
+
+    def weigh_images(i):
+        copies[2 * i + 1].wait()
+        for j in range(READ // 16):
+            rows = slice(16 * j, 16 * j + 16)
             factor = scales[i, rows, :]
             cols = [jnp.broadcast_to(factor[:, c : c + 1], (16, 128)) for c in range(CYC)]
             weighted = []
@@ -207,23 +222,54 @@
                     amount = jnp.where(lane_w < hi * SPAN - 128 * t, cols[lo], cols[hi])
                 pixels = pix[i, rows, 128 * t : 128 * t + 128].astype(jnp.float32)
                 weighted.append((amount * pixels).astype(jnp.bfloat16))
-            for r1 in range(N1):
-                cache = {}
-                plans = rolled_plan(HOP * r1)
-                out_rows = pl.ds(pl.multiple_of(r1 * QP + j * 16, 16), 16)
-                for t in range(TILES):
-                    stack[i, out_rows, 128 * t : 128 * t + 128] = gather_tile(
-                        plans[t], lambda u: weighted[u], lane_w, cache
-                    )
-            return carry
-
-        lax.fori_loop(0, READ // 16, row_step, 0)
-        logits[...] += lax.dot_general(
-            turned[...], stack[i], (((1,), (1,)), ((), ())), preferred_element_type=jnp.float32
+            stack[i, rows, :] = jnp.concatenate(weighted, axis=1)
+
+    def turn_images(i, r1):
+        lane16 = (lane_w + nought[i]).astype(jnp.int16)
+        groups_in = [slice(16 * j, 16 * j + 16) for j in range(READ // 16)]
+        groups_out = [
+            slice(r1 * QP + 16 * j, r1 * QP + 16 * j + 16) for j in range(READ // 16)
+        ]
+        store_tiles(
+            stack.at[i],
+            groups_out,
+            rolled_plan(HOP * r1),
+            lambda g, u: stack[i, groups_in[g], 128 * u : 128 * u + 128],
+            lane16,
         )
-        return energy
-
-    energy = lax.fori_loop(0, CHUNKS, chunk_step, jnp.zeros((K_OWN, CYCLES), jnp.float32))
+
+    def multiply(i, part):
+        cols = slice(2 * QP * part, 2 * QP * (part + 1))
+        value = None
+        for span in (slice(0, 14 * 128), slice(14 * 128, WIDE)):
+            piece = lax.dot_general(
+                turned[i % 2, :, span],
+                stack[i, cols, span],
+                (((1,), (1,)), ((), ())),
+                preferred_element_type=jnp.float32,
+            )
+            value = piece if value is None else value + piece
+        if i:
+            value = value + logits[:, cols]
+        logits[:, cols] = value
+
+    energy = jnp.zeros((K_OWN, CYCLES), jnp.float32)
+    for i in range(CHUNKS):
+        for r1 in range(N1):
+            stack[i, r1 * QP + READ : (r1 + 1) * QP, :] = jnp.zeros(
+                (QP - READ, WIDE), jnp.bfloat16
+            )
+        energy = turn_refs(i, energy)
+        if i:
+            multiply(i - 1, 0)
+        weigh_images(i)
+        for r1 in range(1, N1):
+            if i and r1 in (2, 4):
+                multiply(i - 1, r1 // 2)
+            turn_images(i, r1)
+    for part in range(3):
+        multiply(CHUNKS - 1, part)
+
     ref_power = lax.dot_general(
         energy,
         power,
@@ -266,12 +312,14 @@
     for c in range(CYC):
         for part in range(4):
             total = None
+            masks = {}
             for r2 in range(N2):
                 value = gather_tile(
                     packed_plan(c, part, N1 * HOP * r2),
                     lambda u: partial[r2 * KP : (r2 + 1) * KP, 128 * u : 128 * u + 128],
                     lane,
                     caches[r2],
+                    masks,
                 )
                 total = value if total is None else total + value
             if part == 3:
@@ -364,7 +412,7 @@
         scratch_shapes=[
             pltpu.VMEM((CHUNKS, READ, WIDE), bf16),
             pltpu.VMEM((CHUNKS, K_OWN, WIDE), bf16),
-            pltpu.VMEM((N2 * KP, WIDE), bf16),
+            pltpu.VMEM((2, N2 * KP, WIDE), bf16),
             pltpu.VMEM((CHUNKS, QP, 128), f32),
             pltpu.VMEM((N2 * KP, N1 * QP), f32),
             pltpu.VMEM((24, 128), jnp.int32),

time: 66.4 us -> 61.3 us (0.923)
  Pallas kernels: 27.6 us -> 22.5 us
    pallas_call x1, Pallas kernels: 19.6 us -> 14.5 us  [body(): pl.pallas_call(match_kernel, out_shape=(pltpu.VMEM((CHUNKS, N1 * QP, WIDE...]
where the time goes in v1:
time: 61.3 us; the launch traced here: 60.5 us
  blocking collectives  26.6 us (43%)
  Pallas kernels  22.5 us (37%)
  waiting for transfers between devices  5.52 us (9%)
  starting transfers between devices  5.11 us (8%)
  between operations  0.65 us (1%)
    all_to_all x1, blocking collectives, body(): lax.all_to_all(total.astype(bf16), 'dom', 0, 0, axis_index_groups=z_groups)  17.9 us
    pallas_call x1, Pallas kernels, body(): pl.pallas_call(match_kernel, out_shape=(pltpu.VMEM((CHUNKS, N1 * QP, WIDE...  14.5 us
    all_to_all x1, blocking collectives, body(): stats = lax.all_to_all(stats, 'cls', 0, 0)  8.7 us
    ppermute x3, waiting for transfers between devices, moved(): return lax.ppermute(piece, 'dom', ring)  5.52 us
    ppermute x3, starting transfers between devices, moved(): return lax.ppermute(piece, 'dom', ring)  5.11 us
    pallas_call x3, Pallas kernels, chunk_call(): pl.pallas_call(functools.partial(chunk_kernel, hop), out_shape=jax.ShapeD...  5.01 us
    pallas_call x1, Pallas kernels, body(): pl.pallas_call(functools.partial(first_chunk_kernel, 2), out_shape=(jax.S...  2.19 us
  transfers between devices with their start and end apart: 3, of which 3 were waited for; matrix products, arithmetic and copies ran while one was open for 0% of the time, Pallas kernels for 3%

profile of v1, /device:TPU:8, one launch (start us, length us, event | category | flops | bytes accessed | tf_op | source)
XLA Modules:
  0.0 60.5 jit_solution(16526991667158694364)
XLA Ops:
  0.6 14.5 %match.1 = (bf16[4,768,3456]{2,1,0:T(8,128)(2,1)S(1)}, f32[192,768]{1,0:T(8,128)S(1)}, f32[8,8,128]{2,1,0:T(8,128)S(1)}, f32[128,32]{1,0:T(8,128)S(1)}) custom-call(bf16[96,13824]{1,0:T(8,128)(2,1)} %images.1, bf16[25,13824]{1,0:T(8,128)(2,1)} %refs.1, s32[24,128]{1,0:T(8,128)} %bitcast.3, f32[32,32]{1,0:T(8,128)} %table_far.1, f32[1,32]{1,0:T(1,128)} %bitcast.4, ...), custom_call_target="tpu_custom_call" | custom-call | tf_op jit(solution)/shard_map/match/pallas_call | solution.py:402
  15.1 8.7 %all_to_all.10.stats = f32[8,8,128]{2,1,0:T(8,128)S(1)} all-to-all(f32[8,8,128]{2,1,0:T(8,128)S(1)} %get-tuple-element.12), channel_id=1, replica_groups=mesh['dom'=32,'cls'=8] {'cls'}, dimensions={0} | all-to-all | bytes 65536 | tf_op jit(solution)/shard_map/all_to_all | solution.py:428
  23.8 2.2 %chunk2.1 = (bf16[8,88,128]{2,1,0:T(8,128)(2,1)S(1)}, bf16[192,768]{1,0:T(8,128)(2,1)S(1)}, f32[4,32,128]{2,1,0:T(8,128)S(1)}, f32[1,96]{1,0:T(1,128)}) custom-call(bf16[4,768,3456]{2,1,0:T(8,128)(2,1)S(1)} %get-tuple-element.10.stack, f32[192,768]{1,0:T(8,128)S(1)} %get-tuple-element.11.prob, f32[8,8,128]{2,1,0:T(8,128)S(1)} %all_to_all.10.stats, ...), custom_call_target="tpu_custom_call" | custom-call | tf_op jit(solution)/shard_map/chunk2/pallas_call | solution.py:433
  26.0 1.6 %shard_map.79 = bf16[8,88,128]{2,1,0:T(8,128)(2,1)S(1)} custom-call(bf16[4,768,3456]{2,1,0:T(8,128)(2,1)S(1)} %get-tuple-element.10.stack, bf16[192,768]{1,0:T(8,128)(2,1)S(1)} %get-tuple-element.14.post, f32[4,32,128]{2,1,0:T(8,128)S(1)} %get-tuple-element.15.dens), custom_call_target="tpu_custom_call" | custom-call | tf_op jit(solution)/shard_map/pallas_call | solution.py:454
  27.7 1.7 %shard_map.78 = bf16[8,88,128]{2,1,0:T(8,128)(2,1)S(1)} custom-call(bf16[4,768,3456]{2,1,0:T(8,128)(2,1)S(1)} %get-tuple-element.10.stack, bf16[192,768]{1,0:T(8,128)(2,1)S(1)} %get-tuple-element.14.post, f32[4,32,128]{2,1,0:T(8,128)S(1)} %get-tuple-element.15.dens), custom_call_target="tpu_custom_call" | custom-call | tf_op jit(solution)/shard_map/pallas_call | solution.py:454
  29.4 1.6 %collective-permute-start = (bf16[8,88,128]{2,1,0:T(8,128)(2,1)S(1)}, bf16[8,88,128]{2,1,0:T(8,128)(2,1)S(1)}, u32[]{:S(2)}, u32[]{:S(2)}) collective-permute-start(bf16[8,88,128]{2,1,0:T(8,128)(2,1)S(1)} %shard_map.78), channel_id=1, source_target_pairs={{0,64},{8,72},{16,80},{24,88},{32,96},{40,104},{48,112},{56,120},{... | collective-permute-start | bytes 540680 | tf_op jit(solution)/shard_map/ppermute | solution.py:451
  30.9 1.7 %collective-permute-start.2 = (bf16[8,88,128]{2,1,0:T(8,128)(2,1)S(1)}, bf16[8,88,128]{2,1,0:T(8,128)(2,1)S(1)}, u32[]{:S(2)}, u32[]{:S(2)}) collective-permute-start(bf16[8,88,128]{2,1,0:T(8,128)(2,1)S(1)} %shard_map.79), channel_id=1, source_target_pairs={{0,192},{8,200},{16,208},{24,216},{32,224},{40,232},{48,240},{56,2... | collective-permute-start | bytes 540680 | tf_op jit(solution)/shard_map/ppermute | solution.py:451
  32.7 1.8 %collective-permute-start.1 = (bf16[8,88,128]{2,1,0:T(8,128)(2,1)S(1)}, bf16[8,88,128]{2,1,0:T(8,128)(2,1)S(1)}, u32[]{:S(2)}, u32[]{:S(2)}) collective-permute-start(bf16[8,88,128]{2,1,0:T(8,128)(2,1)S(1)} %get-tuple-element.16), channel_id=1, source_target_pairs={{0,128},{8,136},{16,144},{24,152},{32,160},{40,168},{48,176},{56,1... | collective-permute-start | bytes 540680 | tf_op jit(solution)/shard_map/ppermute | solution.py:451
  34.5 1.7 %shard_map.77 = f32[8,88,128]{2,1,0:T(8,128)S(1)} custom-call(bf16[4,768,3456]{2,1,0:T(8,128)(2,1)S(1)} %get-tuple-element.10.stack, bf16[192,768]{1,0:T(8,128)(2,1)S(1)} %get-tuple-element.14.post, f32[4,32,128]{2,1,0:T(8,128)S(1)} %get-tuple-element.15.dens), custom_call_target="tpu_custom_call" | custom-call | tf_op jit(solution)/shard_map/pallas_call | solution.py:454
  36.2 0.9 %collective-permute-done = bf16[8,88,128]{2,1,0:T(8,128)(2,1)S(1)} collective-permute-done((bf16[8,88,128]{2,1,0:T(8,128)(2,1)S(1)}, bf16[8,88,128]{2,1,0:T(8,128)(2,1)S(1)}, u32[]{:S(2)}, u32[]{:S(2)}) %collective-permute-start) | collective-permute-done | bytes 180256 | tf_op jit(solution)/shard_map/ppermute | solution.py:451
  37.1 2.9 %collective-permute-done.2 = bf16[8,88,128]{2,1,0:T(8,128)(2,1)S(1)} collective-permute-done((bf16[8,88,128]{2,1,0:T(8,128)(2,1)S(1)}, bf16[8,88,128]{2,1,0:T(8,128)(2,1)S(1)}, u32[]{:S(2)}, u32[]{:S(2)}) %collective-permute-start.2) | collective-permute-done | bytes 180256 | tf_op jit(solution)/shard_map/ppermute | solution.py:451
  40.0 1.7 %collective-permute-done.1 = bf16[8,88,128]{2,1,0:T(8,128)(2,1)S(1)} collective-permute-done((bf16[8,88,128]{2,1,0:T(8,128)(2,1)S(1)}, bf16[8,88,128]{2,1,0:T(8,128)(2,1)S(1)}, u32[]{:S(2)}, u32[]{:S(2)}) %collective-permute-start.1) | collective-permute-done | bytes 180256 | tf_op jit(solution)/shard_map/ppermute | solution.py:451
  41.7 0.1 add_convert_fusion
  41.8 17.9 %all_to_all.11.pieces = bf16[8,88,128]{2,1,0:T(8,128)(2,1)S(1)} all-to-all(bf16[8,88,128]{2,1,0:T(8,128)(2,1)S(1)} %add_convert_fusion), channel_id=1, replica_groups={{0,8,16,24,32,40,48,56},{64,72,80,88,96,104,112,120},{128,136,144,152,1..., dimensions={0} | all-to-all | bytes 360448 | tf_op jit(solution)/shard_map/all_to_all | solution.py:469
  59.7 0.8 %finish.1 = f32[25,432]{1,0:T(8,128)} custom-call(bf16[8,88,128]{2,1,0:T(8,128)(2,1)S(1)} %all_to_all.11.pieces), custom_call_target="tpu_custom_call" | custom-call | tf_op jit(solution)/shard_map/finish/pallas_call | solution.py:470
Async XLA Ops:
  29.4 7.8 %collective-permute-start = (bf16[8,88,128]{2,1,0:T(8,128)(2,1)S(1)}, bf16[8,88,128]{2,1,0:T(8,128)(2,1)S(1)}, u32[]{:S(2)}, u32[]{:S(2)}) collective-permute-start(bf16[8,88,128]{2,1,0:T(8,128)(2,1)S(1)} %shard_map.78), channel_id=1, source_target_pairs={{0,64},{8,72},{16,80},{24,88},{32,96},{40,104},{48,112},{56,120},{... | collective-permute-start | bytes 540680 | tf_op jit(solution)/shard_map/ppermute | solution.py:451
  30.9 9.1 %collective-permute-start.2 = (bf16[8,88,128]{2,1,0:T(8,128)(2,1)S(1)}, bf16[8,88,128]{2,1,0:T(8,128)(2,1)S(1)}, u32[]{:S(2)}, u32[]{:S(2)}) collective-permute-start(bf16[8,88,128]{2,1,0:T(8,128)(2,1)S(1)} %shard_map.79), channel_id=1, source_target_pairs={{0,192},{8,200},{16,208},{24,216},{32,224},{40,232},{48,240},{56,2... | collective-permute-start | bytes 540680 | tf_op jit(solution)/shard_map/ppermute | solution.py:451
  32.7 9.0 %collective-permute-start.1 = (bf16[8,88,128]{2,1,0:T(8,128)(2,1)S(1)}, bf16[8,88,128]{2,1,0:T(8,128)(2,1)S(1)}, u32[]{:S(2)}, u32[]{:S(2)}) collective-permute-start(bf16[8,88,128]{2,1,0:T(8,128)(2,1)S(1)} %get-tuple-element.16), channel_id=1, source_target_pairs={{0,128},{8,136},{16,144},{24,152},{32,160},{40,168},{48,176},{56,1... | collective-permute-start | bytes 540680 | tf_op jit(solution)/shard_map/ppermute | solution.py:451

commit v2 on v1

--- a/solution.py
+++ b/solution.py
@@ -146,36 +146,16 @@
             )
         )
     ]
-    for copy in small:
-        copy.start()
     copies = []
     for i in range(CHUNKS):
         span = pl.ds(i * WIDE, WIDE)
         copies.append(pltpu.make_async_copy(refs.at[:, span], raw.at[i], sems.at[0, i]))
         copies.append(pltpu.make_async_copy(images.at[:, span], pix.at[i], sems.at[1, i]))
-    for copy in copies:
+    small[3].start()
+    copies[0].start()
+    for copy in small[:3] + copies[1:]:
         copy.start()
-    for copy in small:
-        copy.wait()
-
-    lane = lax.broadcasted_iota(jnp.int32, (8, QP), 1)
-    base = me * READ
-    row = base // 128
-    off = base - row * 128
-    turn = lax.rem(128 - off, 128)
-    head = jnp.broadcast_to(groups[pl.ds(row, 1), :], (8, QP))
-    tail = jnp.broadcast_to(groups[pl.ds(jnp.minimum(row + 1, 23), 1), :], (8, QP))
-    mine = jnp.where(
-        lane + off < 128, pltpu.roll(head, turn, axis=1), pltpu.roll(tail, turn, axis=1)
-    )
-    hot = (lax.broadcasted_iota(jnp.int32, (QP, QP), 0) == mine[0:1, :]).astype(jnp.float32)
-    hot = hot.T[:, :GROUPS]
-    ctf = jnp.dot(hot, table[...], precision=HIGH, preferred_element_type=jnp.float32)
-    scale = precision[...] * ctf
-    power = precision[...] * jnp.square(ctf)
-    power_out[...] = power
-    for i in range(CHUNKS):
-        scales[i, :, 0:CYC] = scale[:, i * CYC : (i + 1) * CYC]
+    small[3].wait()
 
     lane_r = lax.broadcasted_iota(jnp.int32, (K_OWN, 128), 1)
     lane_e = lax.broadcasted_iota(jnp.int32, (K_OWN, CYCLES), 1)
@@ -253,14 +233,31 @@
             value = value + logits[:, cols]
         logits[:, cols] = value
 
-    energy = jnp.zeros((K_OWN, CYCLES), jnp.float32)
+    energy = turn_refs(0, jnp.zeros((K_OWN, CYCLES), jnp.float32))
+    for copy in small[:3]:
+        copy.wait()
+    lane = lax.broadcasted_iota(jnp.int32, (8, QP), 1)
+    base = me * READ
+    row = base // 128
+    off = base - row * 128
+    turn = lax.rem(128 - off, 128)
+    head = jnp.broadcast_to(groups[pl.ds(row, 1), :], (8, QP))
+    tail = jnp.broadcast_to(groups[pl.ds(jnp.minimum(row + 1, 23), 1), :], (8, QP))
+    mine = jnp.where(
+        lane + off < 128, pltpu.roll(head, turn, axis=1), pltpu.roll(tail, turn, axis=1)
+    )
+    hot = (lax.broadcasted_iota(jnp.int32, (QP, QP), 0) == mine[0:1, :]).astype(jnp.float32)
+    hot = hot.T[:, :GROUPS]
+    ctf = jnp.dot(hot, table[...], precision=HIGH, preferred_element_type=jnp.float32)
+    scale = precision[...] * ctf
+    power = precision[...] * jnp.square(ctf)
+    power_out[...] = power
     for i in range(CHUNKS):
-        for r1 in range(N1):
-            stack[i, r1 * QP + READ : (r1 + 1) * QP, :] = jnp.zeros(
-                (QP - READ, WIDE), jnp.bfloat16
-            )
-        energy = turn_refs(i, energy)
+        scales[i, :, 0:CYC] = scale[:, i * CYC : (i + 1) * CYC]
+
+    for i in range(CHUNKS):
         if i:
+            energy = turn_refs(i, energy)
             multiply(i - 1, 0)
         weigh_images(i)
         for r1 in range(1, N1):
@@ -306,7 +303,10 @@
 
 
 def scatter_chunk(stack, post, dens, partial, out, x_to):
-    partial[...] = jnp.dot(post[...], stack[x_to], preferred_element_type=jnp.float32)
+    rows = [stack[x_to, r1 * QP : r1 * QP + READ, :] for r1 in range(N1)]
+    partial[...] = jnp.dot(
+        post[...], jnp.concatenate(rows, axis=0), preferred_element_type=jnp.float32
+    )
     lane = lax.broadcasted_iota(jnp.int32, (KP, 128), 1)
     caches = [{} for _ in range(N2)]
     for c in range(CYC):
@@ -353,7 +353,7 @@
             cols = slice(r1 * QP, (r1 + 1) * QP)
             value = prob[rows, cols] * factor
             total = total + value
-            post[rows, cols] = value.astype(jnp.bfloat16)
+            post[rows, r1 * READ : (r1 + 1) * READ] = value[:, :READ].astype(jnp.bfloat16)
     den = jnp.dot(total, power[...], precision=HIGH, preferred_element_type=jnp.float32)
     for i in range(CHUNKS):
         dens[i, :, 0:CYC] = den[:, i * CYC : (i + 1) * CYC]
@@ -434,7 +434,7 @@
         functools.partial(first_chunk_kernel, 2),
         out_shape=(
             jax.ShapeDtypeStruct(part_shape, bf16),
-            pltpu.VMEM((N2 * KP, N1 * QP), bf16),
+            pltpu.VMEM((N2 * KP, N1 * READ), bf16),
             pltpu.VMEM((CHUNKS, KP, 128), f32),
             jax.ShapeDtypeStruct((1, READ), f32),
         ),

time: 61.3 us -> 60.4 us (0.985)
  Pallas kernels: 22.5 us -> 21.5 us
where the time goes in v2:
time: 60.4 us; the launch traced here: 59.6 us
  blocking collectives  26.6 us (44%)
  Pallas kernels  21.5 us (36%)
  waiting for transfers between devices  5.71 us (9%)
  starting transfers between devices  5.1 us (8%)
  between operations  0.65 us (1%)
    all_to_all x1, blocking collectives, body(): lax.all_to_all(total.astype(bf16), 'dom', 0, 0, axis_index_groups=z_groups)  17.9 us
    pallas_call x1, Pallas kernels, body(): pl.pallas_call(match_kernel, out_shape=(pltpu.VMEM((CHUNKS, N1 * QP, WIDE...  14 us
    all_to_all x1, blocking collectives, body(): stats = lax.all_to_all(stats, 'cls', 0, 0)  8.7 us
    ppermute x3, waiting for transfers between devices, moved(): return lax.ppermute(piece, 'dom', ring)  5.71 us
    ppermute x3, starting transfers between devices, moved(): return lax.ppermute(piece, 'dom', ring)  5.1 us
    pallas_call x3, Pallas kernels, chunk_call(): pl.pallas_call(functools.partial(chunk_kernel, hop), out_shape=jax.ShapeD...  4.65 us
    pallas_call x1, Pallas kernels, body(): pl.pallas_call(functools.partial(first_chunk_kernel, 2), out_shape=(jax.S...  2.04 us
  transfers between devices with their start and end apart: 3, of which 3 were waited for; matrix products, arithmetic and copies ran while one was open for 0% of the time, Pallas kernels for 3%

profile of v2, /device:TPU:8, one launch (start us, length us, event | category | flops | bytes accessed | tf_op | source)
XLA Modules:
  0.0 59.6 jit_solution(7683774918871070475)
XLA Ops:
  0.6 14.0 %match.1 = (bf16[4,768,3456]{2,1,0:T(8,128)(2,1)S(1)}, f32[192,768]{1,0:T(8,128)S(1)}, f32[8,8,128]{2,1,0:T(8,128)S(1)}, f32[128,32]{1,0:T(8,128)S(1)}) custom-call(bf16[96,13824]{1,0:T(8,128)(2,1)} %images.1, bf16[25,13824]{1,0:T(8,128)(2,1)} %refs.1, s32[24,128]{1,0:T(8,128)} %bitcast.3, f32[32,32]{1,0:T(8,128)} %table_far.1, f32[1,32]{1,0:T(1,128)} %bitcast.4, ...), custom_call_target="tpu_custom_call" | custom-call | tf_op jit(solution)/shard_map/match/pallas_call | solution.py:402
  14.6 8.7 %all_to_all.10.stats = f32[8,8,128]{2,1,0:T(8,128)S(1)} all-to-all(f32[8,8,128]{2,1,0:T(8,128)S(1)} %get-tuple-element.12), channel_id=1, replica_groups=mesh['dom'=32,'cls'=8] {'cls'}, dimensions={0} | all-to-all | bytes 65536 | tf_op jit(solution)/shard_map/all_to_all | solution.py:428
  23.4 2.0 %chunk2.1 = (bf16[8,88,128]{2,1,0:T(8,128)(2,1)S(1)}, bf16[192,576]{1,0:T(8,128)(2,1)S(1)}, f32[4,32,128]{2,1,0:T(8,128)S(1)}, f32[1,96]{1,0:T(1,128)}) custom-call(bf16[4,768,3456]{2,1,0:T(8,128)(2,1)S(1)} %get-tuple-element.10.stack, f32[192,768]{1,0:T(8,128)S(1)} %get-tuple-element.11.prob, f32[8,8,128]{2,1,0:T(8,128)S(1)} %all_to_all.10.stats, ...), custom_call_target="tpu_custom_call" | custom-call | tf_op jit(solution)/shard_map/chunk2/pallas_call | solution.py:433
  25.4 1.5 %shard_map.79 = bf16[8,88,128]{2,1,0:T(8,128)(2,1)S(1)} custom-call(bf16[4,768,3456]{2,1,0:T(8,128)(2,1)S(1)} %get-tuple-element.10.stack, bf16[192,576]{1,0:T(8,128)(2,1)S(1)} %get-tuple-element.14.post, f32[4,32,128]{2,1,0:T(8,128)S(1)} %get-tuple-element.15.dens), custom_call_target="tpu_custom_call" | custom-call | tf_op jit(solution)/shard_map/pallas_call | solution.py:454
  26.9 1.6 %shard_map.78 = bf16[8,88,128]{2,1,0:T(8,128)(2,1)S(1)} custom-call(bf16[4,768,3456]{2,1,0:T(8,128)(2,1)S(1)} %get-tuple-element.10.stack, bf16[192,576]{1,0:T(8,128)(2,1)S(1)} %get-tuple-element.14.post, f32[4,32,128]{2,1,0:T(8,128)S(1)} %get-tuple-element.15.dens), custom_call_target="tpu_custom_call" | custom-call | tf_op jit(solution)/shard_map/pallas_call | solution.py:454
  28.5 1.6 %collective-permute-start = (bf16[8,88,128]{2,1,0:T(8,128)(2,1)S(1)}, bf16[8,88,128]{2,1,0:T(8,128)(2,1)S(1)}, u32[]{:S(2)}, u32[]{:S(2)}) collective-permute-start(bf16[8,88,128]{2,1,0:T(8,128)(2,1)S(1)} %shard_map.78), channel_id=1, source_target_pairs={{0,64},{8,72},{16,80},{24,88},{32,96},{40,104},{48,112},{56,120},{... | collective-permute-start | bytes 540680 | tf_op jit(solution)/shard_map/ppermute | solution.py:451
  30.1 1.7 %collective-permute-start.2 = (bf16[8,88,128]{2,1,0:T(8,128)(2,1)S(1)}, bf16[8,88,128]{2,1,0:T(8,128)(2,1)S(1)}, u32[]{:S(2)}, u32[]{:S(2)}) collective-permute-start(bf16[8,88,128]{2,1,0:T(8,128)(2,1)S(1)} %shard_map.79), channel_id=1, source_target_pairs={{0,192},{8,200},{16,208},{24,216},{32,224},{40,232},{48,240},{56,2... | collective-permute-start | bytes 540680 | tf_op jit(solution)/shard_map/ppermute | solution.py:451
  31.8 1.8 %collective-permute-start.1 = (bf16[8,88,128]{2,1,0:T(8,128)(2,1)S(1)}, bf16[8,88,128]{2,1,0:T(8,128)(2,1)S(1)}, u32[]{:S(2)}, u32[]{:S(2)}) collective-permute-start(bf16[8,88,128]{2,1,0:T(8,128)(2,1)S(1)} %get-tuple-element.16), channel_id=1, source_target_pairs={{0,128},{8,136},{16,144},{24,152},{32,160},{40,168},{48,176},{56,1... | collective-permute-start | bytes 540680 | tf_op jit(solution)/shard_map/ppermute | solution.py:451
  33.6 1.5 %shard_map.77 = f32[8,88,128]{2,1,0:T(8,128)S(1)} custom-call(bf16[4,768,3456]{2,1,0:T(8,128)(2,1)S(1)} %get-tuple-element.10.stack, bf16[192,576]{1,0:T(8,128)(2,1)S(1)} %get-tuple-element.14.post, f32[4,32,128]{2,1,0:T(8,128)S(1)} %get-tuple-element.15.dens), custom_call_target="tpu_custom_call" | custom-call | tf_op jit(solution)/shard_map/pallas_call | solution.py:454
  35.1 1.1 %collective-permute-done = bf16[8,88,128]{2,1,0:T(8,128)(2,1)S(1)} collective-permute-done((bf16[8,88,128]{2,1,0:T(8,128)(2,1)S(1)}, bf16[8,88,128]{2,1,0:T(8,128)(2,1)S(1)}, u32[]{:S(2)}, u32[]{:S(2)}) %collective-permute-start) | collective-permute-done | bytes 180256 | tf_op jit(solution)/shard_map/ppermute | solution.py:451
  36.2 3.0 %collective-permute-done.2 = bf16[8,88,128]{2,1,0:T(8,128)(2,1)S(1)} collective-permute-done((bf16[8,88,128]{2,1,0:T(8,128)(2,1)S(1)}, bf16[8,88,128]{2,1,0:T(8,128)(2,1)S(1)}, u32[]{:S(2)}, u32[]{:S(2)}) %collective-permute-start.2) | collective-permute-done | bytes 180256 | tf_op jit(solution)/shard_map/ppermute | solution.py:451
  39.2 1.7 %collective-permute-done.1 = bf16[8,88,128]{2,1,0:T(8,128)(2,1)S(1)} collective-permute-done((bf16[8,88,128]{2,1,0:T(8,128)(2,1)S(1)}, bf16[8,88,128]{2,1,0:T(8,128)(2,1)S(1)}, u32[]{:S(2)}, u32[]{:S(2)}) %collective-permute-start.1) | collective-permute-done | bytes 180256 | tf_op jit(solution)/shard_map/ppermute | solution.py:451
  40.9 0.1 add_convert_fusion
  41.0 17.9 %all_to_all.11.pieces = bf16[8,88,128]{2,1,0:T(8,128)(2,1)S(1)} all-to-all(bf16[8,88,128]{2,1,0:T(8,128)(2,1)S(1)} %add_convert_fusion), channel_id=1, replica_groups={{0,8,16,24,32,40,48,56},{64,72,80,88,96,104,112,120},{128,136,144,152,1..., dimensions={0} | all-to-all | bytes 360448 | tf_op jit(solution)/shard_map/all_to_all | solution.py:469
  58.8 0.8 %finish.1 = f32[25,432]{1,0:T(8,128)} custom-call(bf16[8,88,128]{2,1,0:T(8,128)(2,1)S(1)} %all_to_all.11.pieces), custom_call_target="tpu_custom_call" | custom-call | tf_op jit(solution)/shard_map/finish/pallas_call | solution.py:470
Async XLA Ops:
  28.5 7.7 %collective-permute-start = (bf16[8,88,128]{2,1,0:T(8,128)(2,1)S(1)}, bf16[8,88,128]{2,1,0:T(8,128)(2,1)S(1)}, u32[]{:S(2)}, u32[]{:S(2)}) collective-permute-start(bf16[8,88,128]{2,1,0:T(8,128)(2,1)S(1)} %shard_map.78), channel_id=1, source_target_pairs={{0,64},{8,72},{16,80},{24,88},{32,96},{40,104},{48,112},{56,120},{... | collective-permute-start | bytes 540680 | tf_op jit(solution)/shard_map/ppermute | solution.py:451
  30.1 9.1 %collective-permute-start.2 = (bf16[8,88,128]{2,1,0:T(8,128)(2,1)S(1)}, bf16[8,88,128]{2,1,0:T(8,128)(2,1)S(1)}, u32[]{:S(2)}, u32[]{:S(2)}) collective-permute-start(bf16[8,88,128]{2,1,0:T(8,128)(2,1)S(1)} %shard_map.79), channel_id=1, source_target_pairs={{0,192},{8,200},{16,208},{24,216},{32,224},{40,232},{48,240},{56,2... | collective-permute-start | bytes 540680 | tf_op jit(solution)/shard_map/ppermute | solution.py:451
  31.8 9.1 %collective-permute-start.1 = (bf16[8,88,128]{2,1,0:T(8,128)(2,1)S(1)}, bf16[8,88,128]{2,1,0:T(8,128)(2,1)S(1)}, u32[]{:S(2)}, u32[]{:S(2)}) collective-permute-start(bf16[8,88,128]{2,1,0:T(8,128)(2,1)S(1)} %get-tuple-element.16), channel_id=1, source_target_pairs={{0,128},{8,136},{16,144},{24,152},{32,160},{40,168},{48,176},{56,1... | collective-permute-start | bytes 540680 | tf_op jit(solution)/shard_map/ppermute | solution.py:451

commit v3 on v2

--- a/solution.py
+++ b/solution.py
@@ -298,8 +298,7 @@
     mass = jnp.sum(mass, axis=0, keepdims=True)
     sub = lax.broadcasted_iota(jnp.int32, (8, QP), 0)
     block = jnp.where(sub == 0, peak, jnp.where(alive[0:1, :], mass, 0.0))
-    for i in range(8):
-        stats[i] = block
+    stats[...] = block
 
 
 def scatter_chunk(stack, post, dens, partial, out, x_to):
@@ -332,18 +331,15 @@
 
 
 def first_chunk_kernel(
-    hop, stack, prob, stats, power, out, post, dens, conf, partial
+    hop, stack, prob, stats, pair, near, far, back, power, out, post, dens, conf, partial
 ):
     me = lax.axis_index("dom")
-    seat = lax.axis_index("cls")
-    peak = stats[0][0:1, :]
-    for i in range(1, 8):
-        peak = jnp.maximum(peak, stats[i][0:1, :])
-    mass = jnp.zeros((1, QP), jnp.float32)
-    for i in range(8):
-        mass = mass + stats[i][1:2, :] * jnp.exp(stats[i][0:1, :] - peak)
+    pairs = (pair, near, far, back)
+    peak = functools.reduce(jnp.maximum, [part[0:1, :] for part in pairs])
+    masses = [part[1:2, :] * jnp.exp(part[0:1, :] - peak) for part in pairs]
+    mass = (masses[0] + masses[1]) + (masses[2] + masses[3])
     alive = mass > 0.0
-    own_peak = stats[seat][0:1, :]
+    own_peak = stats[0:1, :]
     factor = jnp.where(alive, jnp.exp(own_peak - peak) / mass, 0.0)
     conf[...] = jnp.where(alive, 1.0 / mass, 0.0)[:, :READ]
     total = jnp.zeros((KP, QP), jnp.float32)
@@ -404,7 +400,7 @@
         out_shape=(
             pltpu.VMEM((CHUNKS, N1 * QP, WIDE), bf16),
             pltpu.VMEM((N2 * KP, N1 * QP), f32),
-            jax.ShapeDtypeStruct((8, 8, QP), f32),
+            jax.ShapeDtypeStruct((8, QP), f32),
             pltpu.VMEM((QP, CYCLES), f32),
         ),
         in_specs=[FAR] * 6,
@@ -425,7 +421,15 @@
         compiler_params=PARAMS,
         name="match",
     )(*map(in_hbm, operands))
-    stats = lax.all_to_all(stats, "cls", 0, 0)
+
+    def swapped(x, bits):
+        return lax.ppermute(x, "cls", [(j, j ^ bits) for j in range(8)])
+
+    other = swapped(stats, 1)
+    top = jnp.maximum(stats[0:1], other[0:1])
+    both = stats * jnp.exp(stats[0:1] - top) + other * jnp.exp(other[0:1] - top)
+    pair = jnp.where(jnp.arange(8)[:, None] == 0, top, both)
+    seats = [pair] + [swapped(pair, bits) for bits in (2, 4, 6)]
     stack, prob, power = in_vmem(stack), in_vmem(prob), in_vmem(power)
 
     part_shape = (CYC, PACK, 128)
@@ -438,12 +442,12 @@
             pltpu.VMEM((CHUNKS, KP, 128), f32),
             jax.ShapeDtypeStruct((1, READ), f32),
         ),
-        in_specs=[VM, VM, VM, VM],
+        in_specs=[VM] * 8,
         out_specs=(VM, VM, VM, VM),
         scratch_shapes=[partial],
         compiler_params=PARAMS,
         name="chunk2",
-    )(stack, prob, stats, power)
+    )(stack, prob, stats, *seats, power)
     post, dens = in_vmem(post), in_vmem(dens)
 
     def moved(piece, hop):

time: 60.4 us -> 59.5 us (0.985)
  blocking collectives: 26.6 us -> 17.5 us
  waiting for transfers between devices: 5.71 us -> 9.8 us
  starting transfers between devices: 5.1 us -> 8.33 us
    all_to_all x1 -> x0, blocking collectives: 8.7 us -> none  [body(): stats = lax.all_to_all(stats, 'cls', 0, 0)]
    ppermute x0 -> x4, waiting for transfers between devices: none -> 4.74 us  [swapped(): return lax.ppermute(x, 'cls', [(j, j ^ bits) for j in range(8)])]
    ppermute x0 -> x4, starting transfers between devices: none -> 4.35 us  [swapped(): return lax.ppermute(x, 'cls', [(j, j ^ bits) for j in range(8)])]
    ppermute x3, starting transfers between devices: 5.1 us -> 3.97 us  [moved(): return lax.ppermute(piece, 'dom', ring)]
    ppermute x3, waiting for transfers between devices: 5.71 us -> 5.05 us  [moved(): return lax.ppermute(piece, 'dom', ring)]
  transfers between devices with their start and end apart: 3 -> 7, of which waited for: 3 -> 4; matrix products, arithmetic and copies ran while one was open for 0% -> 0% of each run, Pallas kernels for 3% -> 3%
where the time goes in v3:
time: 59.5 us; the launch traced here: 58.3 us
  Pallas kernels  21.9 us (37%)
  blocking collectives  17.5 us (29%)
  waiting for transfers between devices  9.8 us (16%)
  starting transfers between devices  8.33 us (14%)
  between operations  0.67 us (1%)
    all_to_all x1, blocking collectives, body(): lax.all_to_all(total.astype(bf16), 'dom', 0, 0, axis_index_groups=z_groups)  17.5 us
    pallas_call x1, Pallas kernels, body(): pl.pallas_call(match_kernel, out_shape=(pltpu.VMEM((CHUNKS, N1 * QP, WIDE...  14.2 us
    ppermute x3, waiting for transfers between devices, moved(): return lax.ppermute(piece, 'dom', ring)  5.05 us
    pallas_call x3, Pallas kernels, chunk_call(): pl.pallas_call(functools.partial(chunk_kernel, hop), out_shape=jax.ShapeD...  4.85 us
    ppermute x4, waiting for transfers between devices, swapped(): return lax.ppermute(x, 'cls', [(j, j ^ bits) for j in range(8)])  4.74 us
    ppermute x4, starting transfers between devices, swapped(): return lax.ppermute(x, 'cls', [(j, j ^ bits) for j in range(8)])  4.35 us
    ppermute x3, starting transfers between devices, moved(): return lax.ppermute(piece, 'dom', ring)  3.97 us
    pallas_call x1, Pallas kernels, body(): pl.pallas_call(functools.partial(first_chunk_kernel, 2), out_shape=(jax.S...  2.08 us
  transfers between devices with their start and end apart: 7, of which 4 were waited for; matrix products, arithmetic and copies ran while one was open for 0% of the time, Pallas kernels for 3%

profile of v3, /device:TPU:8, one launch (start us, length us, event | category | flops | bytes accessed | tf_op | source)
XLA Modules:
  0.0 58.3 jit_solution(11752465592858203362)
XLA Ops:
  0.6 14.2 %match.1 = (bf16[4,768,3456]{2,1,0:T(8,128)(2,1)S(1)}, f32[192,768]{1,0:T(8,128)S(1)}, f32[8,128]{1,0:T(8,128)S(1)}, f32[128,32]{1,0:T(8,128)S(1)}) custom-call(bf16[96,13824]{1,0:T(8,128)(2,1)} %images.1, bf16[25,13824]{1,0:T(8,128)(2,1)} %refs.1, s32[24,128]{1,0:T(8,128)} %bitcast.9, f32[32,32]{1,0:T(8,128)} %table_far.1, f32[1,32]{1,0:T(1,128)} %bitcast.10, ...), custom_call_target="tpu_custom_call" | custom-call | tf_op jit(solution)/shard_map/match/pallas_call | solution.py:398
  14.8 0.1 collective-permute-start
  14.9 1.1 %collective-permute-done = f32[8,128]{1,0:T(8,128)S(1)} collective-permute-done((f32[8,128]{1,0:T(8,128)S(1)}, f32[8,128]{1,0:T(8,128)S(1)}, u32[]{:S(2)}, u32[]{:S(2)}) %collective-permute-start) | collective-permute-done | bytes 4128 | tf_op jit(solution)/shard_map/ppermute | solution.py:426
  16.1 0.1 add_select_fusion.pair
  16.1 1.6 %collective-permute-start.3 = (f32[8,128]{1,0:T(8,128)S(1)}, f32[8,128]{1,0:T(8,128)S(1)}, u32[]{:S(2)}, u32[]{:S(2)}) collective-permute-start(f32[8,128]{1,0:T(8,128)S(1)} %add_select_fusion.pair), channel_id=1, source_target_pairs={{0,6},{1,7},{2,4},{3,5},{4,2},{5,3},{6,0},{7,1},{8,14},{9,15},{10,... | collective-permute-start | bytes 12296 | tf_op jit(solution)/shard_map/ppermute | solution.py:426
  17.7 2.6 %collective-permute-start.2 = (f32[8,128]{1,0:T(8,128)S(1)}, f32[8,128]{1,0:T(8,128)S(1)}, u32[]{:S(2)}, u32[]{:S(2)}) collective-permute-start(f32[8,128]{1,0:T(8,128)S(1)} %add_select_fusion.pair), channel_id=1, source_target_pairs={{0,4},{1,5},{2,6},{3,7},{4,0},{5,1},{6,2},{7,3},{8,12},{9,13},{10,... | collective-permute-start | bytes 12296 | tf_op jit(solution)/shard_map/ppermute | solution.py:426
  20.4 0.0 collective-permute-start.1
  20.4 0.0 collective-permute-done.3.back
  20.4 2.5 %collective-permute-done.2.far = f32[8,128]{1,0:T(8,128)S(1)} collective-permute-done((f32[8,128]{1,0:T(8,128)S(1)}, f32[8,128]{1,0:T(8,128)S(1)}, u32[]{:S(2)}, u32[]{:S(2)}) %collective-permute-start.2) | collective-permute-done | bytes 4128 | tf_op jit(solution)/shard_map/ppermute | solution.py:426
  22.8 1.1 %collective-permute-done.1.near = f32[8,128]{1,0:T(8,128)S(1)} collective-permute-done((f32[8,128]{1,0:T(8,128)S(1)}, f32[8,128]{1,0:T(8,128)S(1)}, u32[]{:S(2)}, u32[]{:S(2)}) %collective-permute-start.1) | collective-permute-done | bytes 4128 | tf_op jit(solution)/shard_map/ppermute | solution.py:426
  24.0 2.1 %chunk2.1 = (bf16[8,88,128]{2,1,0:T(8,128)(2,1)S(1)}, bf16[192,576]{1,0:T(8,128)(2,1)S(1)}, f32[4,32,128]{2,1,0:T(8,128)S(1)}, f32[1,96]{1,0:T(1,128)}) custom-call(bf16[4,768,3456]{2,1,0:T(8,128)(2,1)S(1)} %get-tuple-element.10.stack, f32[192,768]{1,0:T(8,128)S(1)} %get-tuple-element.11.prob, f32[8,128]{1,0:T(8,128)S(1)} %get-tuple-element.12.stats, ...), custom_call_target="tpu_custom_call" | custom-call | tf_op jit(solution)/shard_map/chunk2/pallas_call | solution.py:437
  26.1 1.6 %shard_map.79 = bf16[8,88,128]{2,1,0:T(8,128)(2,1)S(1)} custom-call(bf16[4,768,3456]{2,1,0:T(8,128)(2,1)S(1)} %get-tuple-element.10.stack, bf16[192,576]{1,0:T(8,128)(2,1)S(1)} %get-tuple-element.14.post, f32[4,32,128]{2,1,0:T(8,128)S(1)} %get-tuple-element.15.dens), custom_call_target="tpu_custom_call" | custom-call | tf_op jit(solution)/shard_map/pallas_call | solution.py:458
  27.7 1.6 %shard_map.78 = bf16[8,88,128]{2,1,0:T(8,128)(2,1)S(1)} custom-call(bf16[4,768,3456]{2,1,0:T(8,128)(2,1)S(1)} %get-tuple-element.10.stack, bf16[192,576]{1,0:T(8,128)(2,1)S(1)} %get-tuple-element.14.post, f32[4,32,128]{2,1,0:T(8,128)S(1)} %get-tuple-element.15.dens), custom_call_target="tpu_custom_call" | custom-call | tf_op jit(solution)/shard_map/pallas_call | solution.py:458
  29.3 0.4 collective-permute-start.4
  29.7 2.9 %collective-permute-start.6 = (bf16[8,88,128]{2,1,0:T(8,128)(2,1)S(1)}, bf16[8,88,128]{2,1,0:T(8,128)(2,1)S(1)}, u32[]{:S(2)}, u32[]{:S(2)}) collective-permute-start(bf16[8,88,128]{2,1,0:T(8,128)(2,1)S(1)} %shard_map.79), channel_id=1, source_target_pairs={{0,192},{8,200},{16,208},{24,216},{32,224},{40,232},{48,240},{56,2... | collective-permute-start | bytes 540680 | tf_op jit(solution)/shard_map/ppermute | solution.py:455
  32.6 0.7 %collective-permute-start.5 = (bf16[8,88,128]{2,1,0:T(8,128)(2,1)S(1)}, bf16[8,88,128]{2,1,0:T(8,128)(2,1)S(1)}, u32[]{:S(2)}, u32[]{:S(2)}) collective-permute-start(bf16[8,88,128]{2,1,0:T(8,128)(2,1)S(1)} %get-tuple-element.16), channel_id=1, source_target_pairs={{0,128},{8,136},{16,144},{24,152},{32,160},{40,168},{48,176},{56,1... | collective-permute-start | bytes 540680 | tf_op jit(solution)/shard_map/ppermute | solution.py:455
  33.3 1.6 %shard_map.77 = f32[8,88,128]{2,1,0:T(8,128)S(1)} custom-call(bf16[4,768,3456]{2,1,0:T(8,128)(2,1)S(1)} %get-tuple-element.10.stack, bf16[192,576]{1,0:T(8,128)(2,1)S(1)} %get-tuple-element.14.post, f32[4,32,128]{2,1,0:T(8,128)S(1)} %get-tuple-element.15.dens), custom_call_target="tpu_custom_call" | custom-call | tf_op jit(solution)/shard_map/pallas_call | solution.py:458
  34.9 5.0 %collective-permute-done.4 = bf16[8,88,128]{2,1,0:T(8,128)(2,1)S(1)} collective-permute-done((bf16[8,88,128]{2,1,0:T(8,128)(2,1)S(1)}, bf16[8,88,128]{2,1,0:T(8,128)(2,1)S(1)}, u32[]{:S(2)}, u32[]{:S(2)}) %collective-permute-start.4) | collective-permute-done | bytes 180256 | tf_op jit(solution)/shard_map/ppermute | solution.py:455
  39.9 0.0 collective-permute-done.6
  39.9 0.0 collective-permute-done.5
  40.0 0.1 add_convert_fusion
  40.1 17.5 %all_to_all.5.pieces = bf16[8,88,128]{2,1,0:T(8,128)(2,1)S(1)} all-to-all(bf16[8,88,128]{2,1,0:T(8,128)(2,1)S(1)} %add_convert_fusion), channel_id=1, replica_groups={{0,8,16,24,32,40,48,56},{64,72,80,88,96,104,112,120},{128,136,144,152,1..., dimensions={0} | all-to-all | bytes 360448 | tf_op jit(solution)/shard_map/all_to_all | solution.py:473
  57.5 0.8 %finish.1 = f32[25,432]{1,0:T(8,128)} custom-call(bf16[8,88,128]{2,1,0:T(8,128)(2,1)S(1)} %all_to_all.5.pieces), custom_call_target="tpu_custom_call" | custom-call | tf_op jit(solution)/shard_map/finish/pallas_call | solution.py:474
  (2 shorter events, 0.0 us)
Async XLA Ops:
  14.8 1.3 %collective-permute-start = (f32[8,128]{1,0:T(8,128)S(1)}, f32[8,128]{1,0:T(8,128)S(1)}, u32[]{:S(2)}, u32[]{:S(2)}) collective-permute-start(f32[8,128]{1,0:T(8,128)S(1)} %get-tuple-element.12.stats), channel_id=1, source_target_pairs={{0,1},{1,0},{2,3},{3,2},{4,5},{5,4},{6,7},{7,6},{8,9},{9,8},{10,11... | collective-permute-start | bytes 12296 | tf_op jit(solution)/shard_map/ppermute | solution.py:426
  16.1 4.3 %collective-permute-start.3 = (f32[8,128]{1,0:T(8,128)S(1)}, f32[8,128]{1,0:T(8,128)S(1)}, u32[]{:S(2)}, u32[]{:S(2)}) collective-permute-start(f32[8,128]{1,0:T(8,128)S(1)} %add_select_fusion.pair), channel_id=1, source_target_pairs={{0,6},{1,7},{2,4},{3,5},{4,2},{5,3},{6,0},{7,1},{8,14},{9,15},{10,... | collective-permute-start | bytes 12296 | tf_op jit(solution)/shard_map/ppermute | solution.py:426
  17.7 5.1 %collective-permute-start.2 = (f32[8,128]{1,0:T(8,128)S(1)}, f32[8,128]{1,0:T(8,128)S(1)}, u32[]{:S(2)}, u32[]{:S(2)}) collective-permute-start(f32[8,128]{1,0:T(8,128)S(1)} %add_select_fusion.pair), channel_id=1, source_target_pairs={{0,4},{1,5},{2,6},{3,7},{4,0},{5,1},{6,2},{7,3},{8,12},{9,13},{10,... | collective-permute-start | bytes 12296 | tf_op jit(solution)/shard_map/ppermute | solution.py:426
  20.4 3.6 %collective-permute-start.1 = (f32[8,128]{1,0:T(8,128)S(1)}, f32[8,128]{1,0:T(8,128)S(1)}, u32[]{:S(2)}, u32[]{:S(2)}) collective-permute-start(f32[8,128]{1,0:T(8,128)S(1)} %add_select_fusion.pair), channel_id=1, source_target_pairs={{0,2},{1,3},{2,0},{3,1},{4,6},{5,7},{6,4},{7,5},{8,10},{9,11},{10,... | collective-permute-start | bytes 12296 | tf_op jit(solution)/shard_map/ppermute | solution.py:426
  29.3 10.6 %collective-permute-start.4 = (bf16[8,88,128]{2,1,0:T(8,128)(2,1)S(1)}, bf16[8,88,128]{2,1,0:T(8,128)(2,1)S(1)}, u32[]{:S(2)}, u32[]{:S(2)}) collective-permute-start(bf16[8,88,128]{2,1,0:T(8,128)(2,1)S(1)} %shard_map.78), channel_id=1, source_target_pairs={{0,64},{8,72},{16,80},{24,88},{32,96},{40,104},{48,112},{56,120},{... | collective-permute-start | bytes 540680 | tf_op jit(solution)/shard_map/ppermute | solution.py:455
  29.7 10.2 %collective-permute-start.6 = (bf16[8,88,128]{2,1,0:T(8,128)(2,1)S(1)}, bf16[8,88,128]{2,1,0:T(8,128)(2,1)S(1)}, u32[]{:S(2)}, u32[]{:S(2)}) collective-permute-start(bf16[8,88,128]{2,1,0:T(8,128)(2,1)S(1)} %shard_map.79), channel_id=1, source_target_pairs={{0,192},{8,200},{16,208},{24,216},{32,224},{40,232},{48,240},{56,2... | collective-permute-start | bytes 540680 | tf_op jit(solution)/shard_map/ppermute | solution.py:455
  32.6 7.3 %collective-permute-start.5 = (bf16[8,88,128]{2,1,0:T(8,128)(2,1)S(1)}, bf16[8,88,128]{2,1,0:T(8,128)(2,1)S(1)}, u32[]{:S(2)}, u32[]{:S(2)}) collective-permute-start(bf16[8,88,128]{2,1,0:T(8,128)(2,1)S(1)} %get-tuple-element.16), channel_id=1, source_target_pairs={{0,128},{8,136},{16,144},{24,152},{32,160},{40,168},{48,176},{56,1... | collective-permute-start | bytes 540680 | tf_op jit(solution)/shard_map/ppermute | solution.py:455
